TPU v7x, 32 devices: a whole 2x2x4 slice. The times are simulated.
32 devices in a mesh: stn: 2 (over x), tm: 16 (over z, y, core).
Axes of the slice: x: 2, y: 2, z: 4, core: 2. Of those that a mesh axis runs over, the one named last changes fastest.
Arguments:
- spectra: bfloat16 [16, 8, 64, 2, 4096], P('stn', None, 'tm'), may hold values from -6 to 6
- flags: int32 [16, 8, 64, 32], P('stn', None, 'tm'), may hold values from 0 to 1, as said below
- poly_index: int32 [16, 8, 64], P('stn', None, 'tm'), may hold values from 0 to 63
- delay_model: float32 [64, 3], replicated, may hold values from -48 to 48
- partner_order: int32 [16], replicated, may hold values from 0 to 15, each once
Outputs:
- fringe: float32 [2, 256, 8, 256], P(None, ('stn', 'tm'))
Inputs may be any that keep to these rules, and one draw needn't show every extreme that they name: `flags`: 1 marks a flagged block; whole blocks of a station can be flagged for the full window. `partner_order`: each station appears once.
All inputs are finite; a program needn't handle non-finite values.
Results may differ from a plain program's by a relative error of at most 0.003.
Values may be sent and summed in bfloat16 or wider, within the bound.
A program may use at most 128 MiB of HBM per device.

v0:
```python
import math

import jax
import jax.numpy as jnp
from jax import lax
from jax.sharding import PartitionSpec as P

LAGS = 256


def rotate(spectra, flags, coeffs, times, total_time):
    channels = spectra.shape[-1]
    blocks = flags.shape[-1]
    moment = times / total_time
    delay = coeffs[..., 0] + coeffs[..., 1] * moment + coeffs[..., 2] * moment * moment
    freq = jnp.arange(channels, dtype=jnp.int32).astype(jnp.float32) * (math.pi / channels)
    phase = delay[..., None] * freq
    cosine = jnp.cos(phase)
    sine = jnp.sin(phase)
    real = spectra[..., 0, :].astype(jnp.float32)
    imag = spectra[..., 1, :].astype(jnp.float32)
    weight = 1.0 - flags.astype(jnp.float32)
    weight = jnp.broadcast_to(weight[..., None], weight.shape + (channels // blocks,)).reshape(
        real.shape
    )
    new_real = weight * (real * cosine + imag * sine)
    new_imag = weight * (imag * cosine - real * sine)
    return jnp.stack([new_real, new_imag], axis=-2).astype(jnp.bfloat16)


def transform(vis, counts, lags):
    rows, periods, _, channels = vis.shape
    blocks = counts.shape[-1]
    scale = 1.0 / jnp.sqrt(jnp.maximum(counts, 1.0))
    normed = vis.reshape(rows, periods, 2, blocks, channels // blocks) * scale[:, :, None, :, None]
    normed = normed.reshape(rows, periods, 2, channels)
    index = jnp.arange(lags, dtype=jnp.int32)
    middle = lags // 2
    delays = jnp.where(index < middle, index - middle, index - middle + 1)
    turns = jnp.arange(channels, dtype=jnp.int32)[:, None] * delays[None, :] % channels
    angle = turns.astype(jnp.float32) * (2.0 * math.pi / channels)
    cosine = jnp.cos(angle)
    sine = jnp.sin(angle)
    highest = lax.Precision.HIGHEST
    real = normed[:, :, 0].reshape(rows * periods, channels)
    imag = normed[:, :, 1].reshape(rows * periods, channels)
    part_real = jnp.dot(real, cosine, precision=highest) + jnp.dot(imag, sine, precision=highest)
    part_imag = jnp.dot(imag, cosine, precision=highest) - jnp.dot(real, sine, precision=highest)
    part_real = part_real.reshape(rows, periods, lags)
    part_imag = part_imag.reshape(rows, periods, lags)
    pidx = jnp.arange(periods, dtype=jnp.int32)
    pturn = pidx[:, None] * pidx[None, :] % periods
    pangle = pturn.astype(jnp.float32) * (2.0 * math.pi / periods)
    pcos = jnp.cos(pangle)
    psin = jnp.sin(pangle)
    out_real = jnp.einsum("rp,npl->nrl", pcos, part_real, precision=highest) + jnp.einsum(
        "rp,npl->nrl", psin, part_imag, precision=highest
    )
    out_imag = jnp.einsum("rp,npl->nrl", pcos, part_imag, precision=highest) - jnp.einsum(
        "rp,npl->nrl", psin, part_real, precision=highest
    )
    factor = 1.0 / math.sqrt(periods * channels)
    return jnp.stack([out_real, out_imag]) * factor


def correlate(mine, theirs):
    mine_real = mine[:, :, :, 0].astype(jnp.float32)[:, None]
    mine_imag = mine[:, :, :, 1].astype(jnp.float32)[:, None]
    their_real = theirs[:, :, :, 0].astype(jnp.float32)[None]
    their_imag = theirs[:, :, :, 1].astype(jnp.float32)[None]
    real = jnp.sum(mine_real * their_real + mine_imag * their_imag, axis=3)
    imag = jnp.sum(mine_imag * their_real - mine_real * their_imag, axis=3)
    return jnp.stack([real, imag], axis=3)


def per_device(spectra, flags, poly_index, delay_model, partner_order):
    local_count, periods, depth, _, channels = spectra.shape
    cycle_size = lax.axis_size("stn")
    time_width = lax.axis_size("tm")
    stations = local_count * cycle_size
    total_time = float(periods * depth * time_width)
    first_time = lax.axis_index("tm") * depth
    times = (
        jnp.arange(periods, dtype=jnp.int32)[:, None] * (depth * time_width)
        + first_time
        + jnp.arange(depth, dtype=jnp.int32)[None, :]
    ).astype(jnp.float32)
    table_rows = delay_model.shape[0]
    onehot = (poly_index[..., None] == jnp.arange(table_rows, dtype=jnp.int32)).astype(jnp.float32)
    coeffs = jnp.dot(onehot.reshape(-1, table_rows), delay_model, precision=lax.Precision.HIGHEST)
    coeffs = coeffs.reshape(local_count, periods, depth, 3)
    rotated = rotate(spectra, flags, coeffs, times, total_time)
    all_flags = lax.all_gather(flags, "stn", axis=0, tiled=True)
    local_weight = 1.0 - flags.astype(jnp.float32)
    all_weight = 1.0 - all_flags.astype(jnp.float32)
    counts = jnp.einsum(
        "apkx,bpkx->abpx", local_weight, all_weight, precision=lax.Precision.HIGHEST
    )
    band = rotated.shape[-1]
    block = correlate(rotated, lax.all_gather(rotated, "stn", axis=0, tiled=True))
    vis_rows = jnp.take(block, partner_order, axis=1).reshape(
        local_count * stations, periods, 2, band
    )
    count_rows = jnp.take(counts, partner_order, axis=1).reshape(
        local_count * stations, periods, counts.shape[-1]
    )
    owned_vis, owned_counts = (
        lax.psum_scatter(vis_rows, "tm", scatter_dimension=0, tiled=True),
        lax.psum_scatter(count_rows, "tm", scatter_dimension=0, tiled=True),
    )
    return transform(owned_vis, owned_counts, LAGS)


def solution(mesh):
    return jax.shard_map(
        per_device,
        mesh=mesh,
        in_specs=(
            P("stn", None, "tm", None, None),
            P("stn", None, "tm", None),
            P("stn", None, "tm"),
            P(),
            P(),
        ),
        out_specs=P(None, ("stn", "tm"), None, None),
        check_vma=False,
    )
```

profile of v0, /device:TPU:0, one launch (start us, length us, event | category | flops | bytes accessed | tf_op | source)
XLA Modules:
  0.0 696.1 jit_solution(13453206611097222274)
XLA Ops:
  7.4 12.9 %fusion.99 = (bf16[8,8,4,1,4096]{4,3,2,1,0:T(2,128)(2,1)}, bf16[8,8,4,1,4096]{4,3,2,1,0:T(2,128)(2,1)}) fusion(bf16[8,8,4,2,4096]{4,3,2,1,0:T(2,128)(2,1)} %param.5), kind=kLoop, calls=%fused_computation.126 | loop fusion | bytes 8388608 | tf_op jit(solution)/shard_map/slice | solution.py:21
  20.7 1.0 fusion.40
  21.8 21.6 %bitcast_convert_fusion.1 = (f32[8,8,4,4096]{3,1,2,0:T(8,128)}, bf16[8,8,4,1,4096]{4,1,3,2,0:T(8,128)(2,1)S(1)}, f32[8,8,4,4096]{3,1,2,0:T(8,128)}, bf16[8,8,4,1,4096]{4,1,3,2,0:T(8,128)(2,1)S(1)}) fusion(bf16[8,8,4,1,4096]{4,3,2,1,0:T(2,128)(2,1)} %get-tuple-element.15, f32[4096]{0:T(1024)S(1)} %convert_multiply_fusion, f32[8,8,4]{1,2,0:T(4,128)S(1)} %bitcast.83, ...), kind=kLoop, calls=%fused_computation.33 | loop fusion | flops 15728640 | bytes 16827392 | tf_op jit(solution)/shard_map/convert_element_type | solution.py:67
  43.3 2.3 pad_maximum_fusion.1
  45.7 0.3 copy.65
  46.0 0.3 copy-done.5
  46.4 7.1 %all_gather.7 = s32[16,8,4,32]{3,1,2,0:T(8,128)S(1)} all-gather(s32[8,8,4,32]{3,1,2,0:T(8,128)S(1)} %copy.63), channel_id=1, replica_groups=mesh['stn'=2,'tm'=16] {'stn'}, dimensions={0}, use_global_device_ids=true | all-gather | bytes 98304 | tf_op jit(solution)/shard_map/all_gather | solution.py:93
  53.5 0.3 copy.64
  53.8 2.2 convolution_bitcast_fusion
  56.1 0.4 copy.66
  56.5 0.6 gather_fusion.1
  57.2 1.0 bitcast_select_fusion.1
  58.2 0.5 reduce-scatter.3.cloned.1.call-start
  58.7 93.8 %all-gather.2.cloned.1.call-done = bf16[16,8,4,2,4096]{4,1,3,2,0:T(8,128)(2,1)} async-done(((bf16[8,8,4,2,4096]{4,1,3,2,0:T(8,128)(2,1)}), bf16[16,8,4,2,4096]{4,1,3,2,0:T(8,128)(2,1)}) %all-gather.2.cloned.1.call-update) | async-done | bytes 8388624 | tf_op jit(solution)/shard_map/all_gather | solution.py:100
  152.5 11.6 %fusion.12 = (f32[16,8,4,4096]{3,1,2,0:T(8,128)}, f32[16,8,4,4096]{3,1,2,0:T(8,128)}) fusion(bf16[16,8,4,2,4096]{4,1,3,2,0:T(8,128)(2,1)} %all-gather.2.cloned.1.call-done), kind=kLoop, calls=%fused_computation.27 | loop fusion | flops 4194304 | bytes 25165824 | tf_op jit(solution)/shard_map/convert_element_type | solution.py:69
  164.1 48.0 %add_reduce_fusion = (f32[8,16,8,4096]{3,2,1,0:T(8,128)}, f32[8,16,8,4096]{3,2,1,0:T(8,128)}) fusion(f32[16,8,4,4096]{3,1,2,0:T(8,128)} %get-tuple-element.14, f32[8,8,4,4096]{3,1,2,0:T(8,128)} %get-tuple-element.11, f32[16,8,4,4096]{3,1,2,0:T(8,128)} %get-tuple-element.13, f32[8,8,4,4096]{3,1,2,0:T(8,128)S(1)} %copy-done.2), kind=kLoop, calls=%fused_computation.3 | loop fusion | flops 125829120 | bytes 58720256 | tf_op jit(solution)/shard_map/reduce_sum | solution.py:71
  212.2 23.0 %pad_maximum_fusion = f32[8,16,8,2,4096]{4,2,3,1,0:T(8,128)} fusion(f32[8,16,8,1,4096]{4,2,3,1,0:T(8,128)} %bitcast.81, f32[8,16,8,1,4096]{4,2,3,1,0:T(8,128)} %bitcast.80), kind=kLoop, calls=%fused_computation.4 | loop fusion | flops 8388608 | bytes 67108864 | tf_op jit(solution)/shard_map/stack | solution.py:73
  235.1 22.9 %gather_fusion = f32[16,8,8,2,4096]{4,2,3,1,0:T(8,128)} fusion(f32[8,16,8,2,4096]{4,2,3,1,0:T(8,128)} %pad_maximum_fusion, s32[1024]{0:T(1024)S(1)} %pad_clamp_fusion), kind=kCustom, calls=%fused_computation | custom fusion | bytes 67108928 | tf_op jit(solution)/shard_map/jit(_take)/gather | solution.py:101
  258.0 12.1 %copy.62 = f32[8,16,8,2,4096]{4,2,3,1,0:T(8,128)S(1)} copy(f32[8,16,8,2,4096]{4,2,3,0,1:T(8,128)} %bitcast.79) | data formatting | bytes 67108864 | tf_op jit(solution)/shard_map/jit(_take)/gather | solution.py:101
  270.1 12.9 %bitcast_select_fusion = f32[128,8,2,4096]{3,1,2,0:T(8,128)} fusion(f32[8,16,8,2,4096]{4,2,3,1,0:T(8,128)S(1)} %copy.62, pred[128]{0:T(512)(128)(4,1)S(1)} %broadcast_in_dim.29), kind=kLoop, calls=%fused_computation.5 | loop fusion | flops 8388608 | bytes 67108992 | tf_op jit(solution)/shard_map/jit(_take)/select_n | solution.py:101
  283.0 0.8 maximum_rsqrt_fusion
  283.9 0.3 broadcast_bitcast_fusion
  284.2 329.3 %reduce-scatter.3.cloned.1.call-done = f32[8,8,2,4096]{3,1,2,0:T(8,128)} async-done(((f32[128,8,2,4096]{3,1,2,0:T(8,128)}), f32[8,8,2,4096]{3,1,2,0:T(8,128)}) %reduce-scatter.3.cloned.1.call-update) | async-done | bytes 2097168 | tf_op jit(solution)/shard_map/reduce_scatter | solution.py:108
  613.5 1.9 broadcast_multiply_fusion
  615.4 17.7 %fusion.20 = f32[64,256]{1,0:T(8,128)S(1)} fusion(s32[256]{0:T(256)S(1)} %fusion.64, f32[8,8,2,4096]{3,1,2,0:T(8,128)S(1)} %broadcast_multiply_fusion), kind=kOutput, calls=%fused_computation.37 | convolution fusion | flops 819986432 | bytes 1115136 | tf_op jit(solution)/shard_map/dot_general | solution.py:47
  633.1 18.0 %fusion.18 = f32[64,256]{1,0:T(8,128)S(1)} fusion(s32[256]{0:T(256)S(1)} %fusion.64, f32[8,8,2,4096]{3,1,2,0:T(8,128)S(1)} %broadcast_multiply_fusion), kind=kOutput, calls=%fused_computation.36 | convolution fusion | flops 819986432 | bytes 1115136 | tf_op jit(solution)/shard_map/dot_general | solution.py:48
  651.1 18.0 %fusion.31 = f32[8,8,256]{2,1,0:T(8,128)S(1)} fusion(f32[64,256]{1,0:T(8,128)S(1)} %fusion.20, s32[256]{0:T(256)S(1)} %fusion.64, f32[8,8,2,4096]{3,1,2,0:T(8,128)S(1)} %broadcast_multiply_fusion), kind=kOutput, calls=%fused_computation.46 | convolution fusion | flops 820002816 | bytes 1180672 | tf_op jit(solution)/shard_map/dot_general | solution.py:47
  669.4 17.7 %fusion.37 = f32[8,8,256]{2,1,0:T(8,128)S(1)} fusion(f32[64,256]{1,0:T(8,128)S(1)} %fusion.18, s32[256]{0:T(256)S(1)} %fusion.64, f32[8,8,2,4096]{3,1,2,0:T(8,128)S(1)} %broadcast_multiply_fusion), kind=kOutput, calls=%fused_computation.48 | convolution fusion | flops 820002816 | bytes 1180672 | tf_op jit(solution)/shard_map/dot_general | solution.py:48
  687.1 0.2 fusion.50
  687.4 0.2 fusion.27
  687.6 0.2 fusion.26
  687.8 0.7 maximum_multiply_fusion
  (34 shorter events, 1.0 us)
Async XLA Ops:
  7.4 13.3 %copy-start = (f32[64,3]{0,1:T(4,128)S(1)}, f32[64,3]{0,1:T(4,128)}, u32[]{:S(2)}) copy-start(f32[64,3]{0,1:T(4,128)} %param.8) | copy-start | bytes 2308
  7.4 145.2 %all-gather.2.cloned.1.call-start = ((), (), s32[]{:S(2)}) async-start(), calls=%async_computation.2 | async-start | bytes 12582912 | tf_op jit(solution)/shard_map/all_gather | solution.py:100
  7.4 13.0 %copy-start.3 = (s32[8,8,4,32]{3,2,1,0:T(4,128)S(1)}, s32[8,8,4,32]{3,2,1,0:T(4,128)}, u32[]{:S(2)}) copy-start(s32[8,8,4,32]{3,2,1,0:T(4,128)} %param.6) | copy-start | bytes 98308
  7.4 13.3 %copy-start.4 = (s32[8,8,4]{1,2,0:T(4,128)S(1)}, s32[8,8,4]{1,2,0:T(4,128)}, u32[]{:S(2)}) copy-start(s32[8,8,4]{1,2,0:T(4,128)} %param.7) | copy-start | bytes 3076
  45.6 0.7 copy-start.5
  45.7 237.4 %reduce-scatter.5.cloned.1.call-start = ((), (), s32[]{:S(2)}) async-start(), calls=%async_computation.4 | async-start | bytes 557056 | tf_op jit(solution)/shard_map/reduce_scatter | solution.py:109
  58.2 555.4 %reduce-scatter.3.cloned.1.call-start = ((), (), s32[]{:S(2)}) async-start(), calls=%async_computation.3 | async-start | bytes 35651584 | tf_op jit(solution)/shard_map/reduce_scatter | solution.py:108
  152.5 11.6 %copy-start.2 = (f32[8,8,4,4096]{3,1,2,0:T(8,128)S(1)}, f32[8,8,4,4096]{3,1,2,0:T(8,128)}, u32[]{:S(2)}) copy-start(f32[8,8,4,4096]{3,1,2,0:T(8,128)} %get-tuple-element.7) | copy-start | bytes 12582916
  669.3 19.2 %copy-start.1 = (f32[64,3]{0,1:T(4,128)S(1)}, f32[64,3]{0,1:T(4,128)}, u32[]{:S(2)}) copy-start(f32[64,3]{0,1:T(4,128)} %param.8) | copy-start | bytes 2308
Sparse Core Ops, SparseCore 0:
  45.8 106.6 all-gather.1
Sparse Core Ops, SparseCore 1:
  58.3 57.7 reduce-scatter.4
  283.1 330.4 reduce-scatter.2
where the time goes:
time: 702 us; the launch traced here: 696 us
  waiting for transfers between devices  423 us (60%)
  other arithmetic  124 us (18%)
  matrix products  75.6 us (11%)
  local copies, waits for them, and re-layouts  50.6 us (7%)
  between operations  15.3 us (2%)
  blocking collectives  7.11 us (1%)
    reduce_scatter x1, waiting for transfers between devices, per_device(): lax.psum_scatter(vis_rows, 'tm', scatter_dimension=0, tiled=True)  329 us
    all_gather x1, waiting for transfers between devices, per_device(): lax.all_gather(rotated, 'stn', axis=0, tiled=True)  93.8 us
    reduce_sum x1, other arithmetic, correlate(): real = jnp.sum(mine_real * their_real + mine_imag * their_imag, axis=3)  48 us
    gather x2, local copies, waits for them, and re-layouts, per_device(): jnp.take(block, partner_order, axis=1)  34.9 us
    another operation x1, other arithmetic, correlate(): return jnp.stack([real, imag], axis=3)  23 us
    convert_element_type x1, other arithmetic, correlate(): mine_real = mine[:, :, :, 0].astype(jnp.float32)[:, None]  21.6 us
    dot_general x1, matrix products, transform(): jnp.dot(imag, cosine, precision=highest)  18 us
    dot_general x1, matrix products, transform(): jnp.dot(imag, sine, precision=highest)  18 us
  transfers between devices with their start and end apart: 3, of which 2 were waited for; matrix products, arithmetic and copies ran while one was open for 20% of the time, Pallas kernels for 0%

commit v1 on v0

v1 whole, which is shorter than its diff:
```python
import functools
import math

import jax
import jax.numpy as jnp
import numpy as np
from jax import lax
from jax.experimental import pallas as pl
from jax.experimental.pallas import tpu as pltpu
from jax.sharding import PartitionSpec as P

LAGS = 256
QUARTERS = 4
LANES = 128


def lag_tables(channels):
    lags = np.arange(1, LAGS // 2 + 1)
    j = np.arange(channels // QUARTERS)
    angle = (j[:, None] * lags[None, :] % channels) * (2.0 * np.pi / channels)
    table = np.concatenate([np.cos(angle), np.sin(angle)], axis=1).astype(np.float32)
    high = table.astype(jnp.bfloat16)
    low = (table - high.astype(np.float32)).astype(jnp.bfloat16)
    return high, low


def split(value):
    high = value.astype(jnp.bfloat16)
    low = (value - high.astype(jnp.float32)).astype(jnp.bfloat16)
    return high, low


def dot(a, b):
    return jnp.dot(a, b, preferred_element_type=jnp.float32)


def correlate_kernel(x_ref, e1_ref, e2_ref, scale_ref, wh_ref, wl_ref, pick_ref, out_ref, y_ref, vh_ref, vl_ref, z_ref):
    depth, _, stations, width = x_ref.shape[1:]
    half = stations // 2
    blocks = width // LANES
    quarter = pl.program_id(1)

    def put(row, col, value):
        high, low = split(value)
        cols = slice(col * LANES, (col + 1) * LANES)
        vh_ref[row : row + stations, cols] = high
        vl_ref[row : row + stations, cols] = low

    for h in range(blocks):
        cols = slice(h * LANES, (h + 1) * LANES)
        slot = h % 2
        mine = []
        for k in range(depth):
            c1 = e1_ref[0, 0, k, 0, :, h : h + 1]
            s1 = e1_ref[0, 0, k, 1, :, h : h + 1]
            c2 = e2_ref[0, k, 0]
            s2 = e2_ref[0, k, 1]
            cosine = c1 * c2 - s1 * s2
            sine = s1 * c2 + c1 * s2
            real = x_ref[0, k, 0, :, cols].astype(jnp.float32)
            imag = x_ref[0, k, 1, :, cols].astype(jnp.float32)
            new_real = (real * cosine + imag * sine).astype(jnp.bfloat16).astype(jnp.float32)
            new_imag = (imag * cosine - real * sine).astype(jnp.bfloat16).astype(jnp.float32)
            y_ref[slot, k, 0, :stations] = new_real
            y_ref[slot, k, 1, :stations] = new_imag
            y_ref[slot, k, 0, stations:] = new_real[:half]
            y_ref[slot, k, 1, stations:] = new_imag[:half]
            mine.append((new_real, new_imag))
        for d in range(half + 1):
            count = half if d == half else stations
            real = None
            imag = None
            for k in range(depth):
                ar, ai = mine[k]
                ar, ai = ar[:count], ai[:count]
                if d == 0:
                    br, bi = ar, ai
                else:
                    br = y_ref[slot, k, 0, d : d + count]
                    bi = y_ref[slot, k, 1, d : d + count]
                term = ar * br + ai * bi
                real = term if real is None else real + term
                if d > 0:
                    term = ai * br - ar * bi
                    imag = term if imag is None else imag + term
            scale = scale_ref[0, 0, d * stations : d * stations + count, h : h + 1]
            if d == half:
                both = jnp.concatenate([real * scale, imag * scale], axis=0)
                put(stations * (stations - 1), h, both)
            else:
                put(d * stations, h, real * scale)
                if d > 0:
                    put((half + d - 1) * stations, h, imag * scale)

    vh = vh_ref[...]
    part = dot(vh, wh_ref[...]) + dot(vh, wl_ref[...]) + dot(vl_ref[...], wh_ref[...])
    lags = part.shape[1] // 2
    part_c = part[:, :lags]
    part_s = part[:, lags:]
    lag = lax.broadcasted_iota(jnp.int32, part_c.shape, 1) + 1
    turn = (lag * quarter) % 4
    cq = jnp.where(turn == 0, 1.0, jnp.where(turn == 2, -1.0, 0.0))
    sq = jnp.where(turn == 1, 1.0, jnp.where(turn == 3, -1.0, 0.0))
    new_c = part_c * cq - part_s * sq
    new_s = part_s * cq + part_c * sq

    @pl.when(quarter == 0)
    def _():
        z_ref[:, :lags] = new_c
        z_ref[:, lags:] = new_s

    @pl.when(quarter > 0)
    def _():
        z_ref[:, :lags] += new_c
        z_ref[:, lags:] += new_s

    @pl.when(quarter == QUARTERS - 1)
    def _():
        z = z_ref[...]
        high = z.astype(jnp.bfloat16)
        rest = z - high.astype(jnp.float32)
        mid, low = split(rest)
        pick = pick_ref[...]
        rows = dot(pick, high) + dot(pick, mid) + dot(pick, low)
        out_ref[...] = rows.reshape(out_ref.shape)


def correlate(x, e1, e2, scale, high, low, pick, owners):
    periods, depth, _, stations, channels = x.shape
    width = channels // QUARTERS
    rows = stations * stations
    return pl.pallas_call(
        correlate_kernel,
        grid=(periods, QUARTERS),
        in_specs=[
            pl.BlockSpec((1, depth, 2, stations, width), lambda p, q: (p, 0, 0, 0, q)),
            pl.BlockSpec((1, 1) + e1.shape[2:], lambda p, q: (p, q, 0, 0, 0, 0)),
            pl.BlockSpec((1,) + e2.shape[1:], lambda p, q: (p, 0, 0, 0, 0)),
            pl.BlockSpec((1, 1) + scale.shape[2:], lambda p, q: (p, q, 0, 0)),
            pl.BlockSpec(high.shape, lambda p, q: (0, 0)),
            pl.BlockSpec(low.shape, lambda p, q: (0, 0)),
            pl.BlockSpec(pick.shape, lambda p, q: (0, 0)),
        ],
        out_specs=pl.BlockSpec((owners, 1, 2 * rows // owners, LAGS), lambda p, q: (0, p, 0, 0)),
        out_shape=jax.ShapeDtypeStruct((owners, periods, 2 * rows // owners, LAGS), jnp.float32),
        scratch_shapes=[
            pltpu.VMEM((2, depth, 2, stations + stations // 2, LANES), jnp.float32),
            pltpu.VMEM((rows, width), jnp.bfloat16),
            pltpu.VMEM((rows, width), jnp.bfloat16),
            pltpu.VMEM((rows, LAGS), jnp.float32),
        ],
        compiler_params=pltpu.CompilerParams(dimension_semantics=("arbitrary", "arbitrary")),
        name="correlate",
    )(x, e1, e2, scale, high, low, pick)


def finish_kernel(factor, g_ref, pc_ref, ps_ref, out_ref):
    highest = lax.Precision.HIGHEST
    lags = g_ref.shape[-1] // 2
    rc, rs = g_ref[0, :, :lags], g_ref[0, :, lags:]
    ic, im_s = g_ref[1, :, :lags], g_ref[1, :, lags:]
    flip = (
        lax.broadcasted_iota(jnp.int32, (lags, lags), 0) + lax.broadcasted_iota(jnp.int32, (lags, lags), 1) == lags - 1
    ).astype(jnp.float32)
    pcos = pc_ref[...]
    psin = ps_ref[...]

    def mix(m, v):
        return jnp.dot(m, v, precision=highest, preferred_element_type=jnp.float32)

    for side in range(2):
        if side == 0:
            real, imag = mix(rc - im_s, flip), mix(ic + rs, flip)
        else:
            real, imag = rc + im_s, ic - rs
        cols = slice(side * lags, (side + 1) * lags)
        out_ref[0, :, cols] = (mix(pcos, real) + mix(psin, imag)) * factor
        out_ref[1, :, cols] = (mix(pcos, imag) - mix(psin, real)) * factor


def finish(g, periods, channels):
    rows = g.shape[1] // periods
    idx = np.arange(periods)
    angle = (idx[:, None] * idx[None, :] % periods) * (2.0 * np.pi / periods)
    eye = np.eye(rows)

    def table(m):
        wide = np.einsum("rp,nm->nrpm", m, eye).reshape(rows * periods, periods * rows)
        return jnp.asarray(wide.astype(np.float32))

    out = pl.pallas_call(
        functools.partial(finish_kernel, 1.0 / math.sqrt(periods * channels)),
        out_shape=jax.ShapeDtypeStruct((2, rows * periods, LAGS), jnp.float32),
        name="finish",
    )(g, table(np.cos(angle)), table(np.sin(angle)))
    return out.reshape(2, rows, periods, LAGS)


def pick_matrix(partner_order, stations, first_station, groups, owners):
    half = stations // 2
    own_rows = stations * stations // (groups * owners)
    n = np.arange(stations * stations).reshape(groups, owners, own_rows).transpose(1, 0, 2)
    a = jnp.asarray(n // stations, jnp.int32)
    onehot = (jnp.asarray(n % stations, jnp.int32)[..., None] == jnp.arange(stations)).astype(jnp.int32)
    b = jnp.sum(onehot * partner_order, axis=-1)
    a = (a - first_station) % stations
    b = (b - first_station) % stations
    d = (b - a) % stations
    flip = (d > half) | ((d == half) & (a >= half))
    d = jnp.where(flip, (stations - d) % stations, d)
    row = jnp.where(flip, b, a)
    top = stations * (stations - 1)
    real_col = jnp.where(d == half, top + row, d * stations + row)
    imag_col = jnp.where(d == half, top + half + row, (half + d - 1) * stations + row)
    imag_col = jnp.where(d == 0, -1, imag_col)
    sign = jnp.where(flip, -1.0, 1.0)
    col = jnp.stack([real_col, imag_col], axis=2)
    value = jnp.stack([jnp.ones_like(sign), sign], axis=2)
    pick = jnp.where(col[..., None] == jnp.arange(stations * stations), value[..., None], 0.0)
    return pick.reshape(2 * stations * stations, stations * stations).astype(jnp.bfloat16)


def per_device(spectra, flags, poly_index, delay_model, partner_order):
    local, periods, depth, _, channels = spectra.shape
    groups = lax.axis_size("stn")
    owners = lax.axis_size("tm")
    me = lax.axis_index("stn")
    stations = local * groups
    mine = periods // groups
    blocks = flags.shape[-1]
    first_station = (me + 1) % groups * local

    chunks = []
    for i in range(mine):
        pieces = []
        for shift in range(groups - 1, -1, -1):
            target = (me + shift) % groups
            piece = lax.dynamic_slice_in_dim(spectra, target * mine + i, 1, axis=1)
            if shift:
                piece = lax.ppermute(piece, "stn", [(g, (g + shift) % groups) for g in range(groups)])
            pieces.append(piece)
        chunks.append(jnp.concatenate(pieces, axis=0).transpose(1, 2, 3, 0, 4))

    ints = jnp.concatenate([flags, poly_index[..., None]], axis=-1)
    ints = lax.all_to_all(ints, "stn", split_axis=1, concat_axis=0, tiled=True)
    ints = jnp.roll(ints, -first_station, axis=0)
    weight = 1.0 - ints[..., :blocks].astype(jnp.float32)
    index = ints[..., blocks]

    pairs = jnp.stack([weight * jnp.roll(weight, -d, axis=0) for d in range(stations // 2 + 1)])
    counts = jnp.sum(pairs, axis=3).reshape((stations // 2 + 1) * stations, mine, blocks)
    counts = lax.psum(counts.astype(jnp.bfloat16), "tm").astype(jnp.float32)
    scale = 1.0 / jnp.sqrt(jnp.maximum(counts, 1.0))
    scale = scale.reshape(scale.shape[0], mine, QUARTERS, blocks // QUARTERS).transpose(1, 2, 0, 3)

    total = depth * owners
    times = (
        (me * mine + jnp.arange(mine, dtype=jnp.int32))[:, None] * total
        + lax.axis_index("tm") * depth
        + jnp.arange(depth, dtype=jnp.int32)[None, :]
    ).astype(jnp.float32)
    moment = times / float(periods * total)
    table_rows = delay_model.shape[0]
    onehot = (index[..., None] == jnp.arange(table_rows, dtype=jnp.int32)).astype(jnp.float32)
    coeffs = jnp.dot(onehot.reshape(-1, table_rows), delay_model, precision=lax.Precision.HIGHEST)
    coeffs = coeffs.reshape(stations, mine, depth, 3)
    delay = coeffs[..., 0] + coeffs[..., 1] * moment + coeffs[..., 2] * moment * moment
    step = math.pi / channels
    coarse = delay[..., None] * (jnp.arange(blocks, dtype=jnp.int32).astype(jnp.float32) * (step * (channels // blocks)))
    fine = delay[..., None] * (jnp.arange(channels // blocks, dtype=jnp.int32).astype(jnp.float32) * step)
    e1 = jnp.stack([weight * jnp.cos(coarse), weight * jnp.sin(coarse)], axis=3)
    e1 = e1.reshape(stations, mine, depth, 2, QUARTERS, blocks // QUARTERS).transpose(1, 4, 2, 3, 0, 5)
    e2 = jnp.stack([jnp.cos(fine), jnp.sin(fine)], axis=3).transpose(1, 2, 3, 0, 4)

    high, low = lag_tables(channels)
    high, low = jnp.asarray(high), jnp.asarray(low)
    pick = pick_matrix(partner_order, stations, first_station, groups, owners)
    done = []
    for i in range(mine):
        part = correlate(chunks[i], e1[i : i + 1], e2[i : i + 1], scale[i : i + 1], high, low, pick, owners)
        done.append(lax.psum_scatter(part, "tm", scatter_dimension=0, tiled=True)[0])
    own = jnp.concatenate(done, axis=0)
    own = own.reshape(mine, groups, 2, -1, LAGS)
    own = lax.all_to_all(own, "stn", split_axis=1, concat_axis=0, tiled=True)
    own = own.reshape(periods, 2, -1, LAGS).transpose(1, 0, 2, 3).reshape(2, -1, LAGS)
    return finish(own, periods, channels)


def solution(mesh):
    return jax.shard_map(
        per_device,
        mesh=mesh,
        in_specs=(
            P("stn", None, "tm", None, None),
            P("stn", None, "tm", None),
            P("stn", None, "tm"),
            P(),
            P(),
        ),
        out_specs=P(None, ("stn", "tm"), None, None),
        check_vma=False,
    )
```

time: 702 us -> 358 us (0.51)
  waiting for transfers between devices: 423 us -> 194 us
  other arithmetic: 124 us -> 11.8 us
  matrix products: 75.6 us -> 0.62 us
  blocking collectives: 7.11 us -> 68.6 us
  Pallas kernels: 0 us -> 38.3 us
  local copies, waits for them, and re-layouts: 50.6 us -> 21.2 us
  starting transfers between devices: 0.55 us -> 8.81 us
    reduce_scatter x2 -> x4, waiting for transfers between devices: 329 us -> 194 us  [per_device(): lax.psum_scatter(part, 'tm', scatter_dimension=0, tiled=True)[0]]
    all_gather x1 -> x0, waiting for transfers between devices: 93.8 us -> none  [per_device(): lax.all_gather(rotated, 'stn', axis=0, tiled=True)]
    dot_general x9 -> x0, matrix products: 74.6 us -> none  [the longest x1 18 us: transform(): jnp.dot(imag, cosine, precision=highest)]
    psum x0 -> x1, blocking collectives: none -> 61.6 us  [per_device(): counts = lax.psum(counts.astype(jnp.bfloat16), 'tm').astype(jnp.float32)]
    reduce_sum x1 -> x2, other arithmetic: 48 us -> 0.84 us  [the longest x1 0.73 us: pick_matrix(): b = jnp.sum(onehot * partner_order, axis=-1)]
    pallas_call x0 -> x5, Pallas kernels: none -> 38.3 us  [the longest x4 36.2 us: correlate(): pl.pallas_call(correlate_kernel, grid=(periods, QUARTERS), in_specs=[pl.B...]
    gather x4 -> x0, local copies, waits for them, and re-layouts: 35.6 us -> none  [the longest x2 34.9 us: per_device(): jnp.take(block, partner_order, axis=1)]
    convert_element_type x2 -> x1, other arithmetic: 33.2 us -> 0.92 us  [pick_matrix(): pick.reshape(2 * stations * stations, stations * stations)]
  transfers between devices with their start and end apart: 3 -> 9, of which waited for: 2 -> 4; matrix products, arithmetic and copies ran while one was open for 20% -> 8% of each run, Pallas kernels for 0% -> 10%
where the time goes in v1:
time: 358 us; the launch traced here: 357 us
  waiting for transfers between devices  194 us (54%)
  blocking collectives  68.6 us (19%)
  Pallas kernels  38.3 us (11%)
  local copies, waits for them, and re-layouts  21.2 us (6%)
  between operations  13.6 us (4%)
  other arithmetic  11.8 us (3%)
  starting transfers between devices  8.81 us (2%)
    reduce_scatter x4, waiting for transfers between devices, per_device(): lax.psum_scatter(part, 'tm', scatter_dimension=0, tiled=True)[0]  194 us
    psum x1, blocking collectives, per_device(): counts = lax.psum(counts.astype(jnp.bfloat16), 'tm').astype(jnp.float32)  61.6 us
    pallas_call x4, Pallas kernels, correlate(): pl.pallas_call(correlate_kernel, grid=(periods, QUARTERS), in_specs=[pl.B...  36.2 us
    dynamic_slice x1, local copies, waits for them, and re-layouts, per_device(): piece = lax.dynamic_slice_in_dim(spectra, target * mine + i, 1, axis=1)  7.88 us
  transfers between devices with their start and end apart: 9, of which 4 were waited for; matrix products, arithmetic and copies ran while one was open for 8% of the time, Pallas kernels for 10%

profile of v1, /device:TPU:0, one launch (start us, length us, event | category | flops | bytes accessed | tf_op | source)
XLA Modules:
  0.0 357.1 jit_solution(2376357880272823090)
XLA Ops:
  6.5 1.0 copy.131
  7.5 1.0 copy.132
  8.6 0.9 reshape.105
  9.5 4.2 %all-to-all-start = ((s32[2,1,4224]{2,1,0:T(1,128)}), s32[2,1,4224]{2,1,0:T(1,128)S(1)}, u32[]{:S(2)}, u32[]{:S(2)}) async-start(s32[2,1,4224]{2,1,0:T(1,128)} %reshape.105), calls=%async_computation | async-start | bytes 67584 | tf_op jit(solution)/shard_map/all_to_all | solution.py:245
  13.7 7.9 %constant_dynamic-slice_fusion.7 = (bf16[8,1,4,2,4096]{4,3,2,1,0:T(2,128)(2,1)S(1)}, bf16[8,1,4,2,4096]{4,3,2,1,0:T(2,128)(2,1)}, bf16[8,1,4,2,4096]{4,3,2,1,0:T...) fusion(bf16[8,8,4,2,4096]{4,3,2,1,0:T(2,128)(2,1)} %param.11, ...), kind=kLoop, calls=%fused_computation.92 | loop fusion | bytes 8388640 | tf_op jit(solution)/shard_map/dynamic_slice | solution.py:238
  21.6 1.1 copy.157
  22.7 2.1 collective-permute-start
  24.8 1.1 copy.159
  26.0 0.7 select_reduce_fusion
  27.3 0.9 select_convert_fusion.pick_ref
  29.1 0.7 reduce.2
  32.7 61.6 %psum.7 = bf16[144,4,32]{0,2,1:T(8,128)(2,1)S(1)} all-reduce(bf16[144,4,32]{0,2,1:T(8,128)(2,1)S(1)} %copy.139), channel_id=1, replica_groups=mesh['stn'=2,'tm'=16] {'tm'}, use_global_device_ids=true, to_apply=%region_1.2 | all-reduce | flops 18432 | bytes 73728 | tf_op jit(solution)/shard_map/psum | solution.py:252
  95.7 0.7 fusion.34
  96.9 1.0 fusion.33
  97.9 1.1 fusion.32
  99.0 2.1 maximum_bitcast_fusion.x_ref
  101.1 9.1 %correlate.4 = f32[16,1,32,256]{3,2,1,0:T(8,128)} custom-call(bf16[1,4,2,16,4096]{4,3,2,1,0:T(8,128)(2,1)} %maximum_bitcast_fusion.x_ref, f32[1,4,4,2,16,8]{5,4,3,2,1,0:T(8,128)} %get-tuple-element.21.e1_ref, f32[1,4,2,16,128]{4,3,2,1,0:T(8,128)} %get-tuple-element.25.e2_ref, f32[1,4,144,8]{3,2,1,0:T(8,128)} %get-tuple-element.17.scale_ref, ...), custom_call_target="tpu_custom_call" | custom-call | tf_op jit(solution)/shard_map/correlate/pallas_call | solution.py:132
  110.8 1.7 collective-permute-start.2
  112.7 2.1 maximum_bitcast_fusion.2.x_ref
  114.9 9.1 %correlate.5 = f32[16,1,32,256]{3,2,1,0:T(8,128)} custom-call(bf16[1,4,2,16,4096]{4,3,2,1,0:T(8,128)(2,1)} %maximum_bitcast_fusion.2.x_ref, f32[1,4,4,2,16,8]{5,4,3,2,1,0:T(8,128)} %get-tuple-element.24.e1_ref, f32[1,4,2,16,128]{4,3,2,1,0:T(8,128)} %get-tuple-element.28.e2_ref, f32[1,4,144,8]{3,2,1,0:T(8,128)} %get-tuple-element.20.scale_ref, ...), custom_call_target="tpu_custom_call" | custom-call | tf_op jit(solution)/shard_map/correlate/pallas_call | solution.py:132
  125.3 1.0 maximum_bitcast_fusion.3.x_ref
  126.4 9.0 %correlate.6 = f32[16,1,32,256]{3,2,1,0:T(8,128)} custom-call(bf16[1,4,2,16,4096]{4,3,2,1,0:T(8,128)(2,1)} %maximum_bitcast_fusion.3.x_ref, f32[1,4,4,2,16,8]{5,4,3,2,1,0:T(8,128)} %get-tuple-element.23.e1_ref, f32[1,4,2,16,128]{4,3,2,1,0:T(8,128)} %get-tuple-element.27.e2_ref, f32[1,4,144,8]{3,2,1,0:T(8,128)} %get-tuple-element.19.scale_ref, ...), custom_call_target="tpu_custom_call" | custom-call | tf_op jit(solution)/shard_map/correlate/pallas_call | solution.py:132
  135.8 1.0 maximum_bitcast_fusion.4.x_ref
  136.8 9.0 %correlate.7 = f32[16,1,32,256]{3,2,1,0:T(8,128)} custom-call(bf16[1,4,2,16,4096]{4,3,2,1,0:T(8,128)(2,1)} %maximum_bitcast_fusion.4.x_ref, f32[1,4,4,2,16,8]{5,4,3,2,1,0:T(8,128)} %get-tuple-element.22.e1_ref, f32[1,4,2,16,128]{4,3,2,1,0:T(8,128)} %get-tuple-element.26.e2_ref, f32[1,4,144,8]{3,2,1,0:T(8,128)} %get-tuple-element.18.scale_ref, ...), custom_call_target="tpu_custom_call" | custom-call | tf_op jit(solution)/shard_map/correlate/pallas_call | solution.py:132
  145.8 18.0 %reduce-scatter.5.cloned.1.call-done = f32[1,1,32,256]{3,2,1,0:T(8,128)} async-done(((f32[16,1,32,256]{3,2,1,0:T(8,128)}), f32[1,1,32,256]{3,2,1,0:T(8,128)}) %reduce-scatter.5.cloned.1.call-update) | async-done | bytes 32784 | tf_op jit(solution)/shard_map/reduce_scatter | solution.py:281
  163.9 58.7 %reduce-scatter.7.cloned.1.call-done = f32[1,1,32,256]{3,2,1,0:T(8,128)} async-done(((f32[16,1,32,256]{3,2,1,0:T(8,128)}), f32[1,1,32,256]{3,2,1,0:T(8,128)}) %reduce-scatter.7.cloned.1.call-update) | async-done | bytes 32784 | tf_op jit(solution)/shard_map/reduce_scatter | solution.py:281
  222.6 58.7 %reduce-scatter.9.cloned.1.call-done = f32[1,1,32,256]{3,2,1,0:T(8,128)} async-done(((f32[16,1,32,256]{3,2,1,0:T(8,128)}), f32[1,1,32,256]{3,2,1,0:T(8,128)}) %reduce-scatter.9.cloned.1.call-update) | async-done | bytes 32784 | tf_op jit(solution)/shard_map/reduce_scatter | solution.py:281
  281.3 58.6 %reduce-scatter.11.cloned.1.call-done = f32[1,1,32,256]{3,2,1,0:T(8,128)} async-done(((f32[16,1,32,256]{3,2,1,0:T(8,128)}), f32[1,1,32,256]{3,2,1,0:T(8,128)}) %reduce-scatter.11.cloned.1.call-update) | async-done | bytes 32784 | tf_op jit(solution)/shard_map/reduce_scatter | solution.py:281
  340.0 0.8 pad_maximum_fusion
  340.8 7.0 %all_to_all.33 = f32[4,2,2,8,256]{4,3,2,0,1:T(8,128)S(1)} all-to-all(f32[4,2,2,8,256]{4,3,2,0,1:T(8,128)S(1)} %pad_maximum_fusion), channel_id=1, replica_groups=mesh['stn'=2,'tm'=16] {'stn'}, dimensions={1} | all-to-all | bytes 262144 | tf_op jit(solution)/shard_map/all_to_all | solution.py:284
  347.8 0.7 copy_bitcast_fusion.g_ref
  348.4 2.2 finish.1
  (94 shorter events, 8.6 us)
Async XLA Ops:
  6.5 24.0 %copy-start = (f32[64,3]{0,1:T(4,128)S(1)}, f32[64,3]{0,1:T(4,128)}, u32[]{:S(2)}) copy-start(f32[64,3]{0,1:T(4,128)} %param.14) | copy-start | bytes 2308
  9.5 19.1 %all-to-all-start = ((s32[2,1,4224]{2,1,0:T(1,128)}), s32[2,1,4224]{2,1,0:T(1,128)S(1)}, u32[]{:S(2)}, u32[]{:S(2)}) async-start(s32[2,1,4224]{2,1,0:T(1,128)} %reshape.105), calls=%async_computation | async-start | bytes 67584 | tf_op jit(solution)/shard_map/all_to_all | solution.py:245
  13.7 150.2 %reduce-scatter.5.cloned.1.call-start = ((), (), s32[]{:S(2)}) async-start(), calls=%async_computation.6 | async-start | bytes 557056 | tf_op jit(solution)/shard_map/reduce_scatter | solution.py:281
  21.6 4.4 %copy-start.5 = (s32[16,2,8]{2,1,0:T(2,128)S(1)}, s32[16,2,8]{2,1,0:T(2,128)}, u32[]{:S(2)}) copy-start(s32[16,2,8]{2,1,0:T(2,128)} %constant.149.clone) | copy-start | bytes 3076
  21.6 4.4 %copy-start.7 = (s32[16]{0:T(128)S(1)}, s32[16]{0:T(128)}, u32[]{:S(2)}) copy-start(s32[16]{0:T(128)} %param.15) | copy-start | bytes 196
  21.6 5.1 %copy-start.6 = (s32[16,2,8]{2,1,0:T(2,128)S(1)}, s32[16,2,8]{2,1,0:T(2,128)}, u32[]{:S(2)}) copy-start(s32[16,2,8]{2,1,0:T(2,128)} %constant.148.clone) | copy-start | bytes 3076
  22.7 76.3 %collective-permute-start = (bf16[8,1,4,2,4096]{4,0,3,2,1:T(8,128)(2,1)}, bf16[8,1,4,2,4096]{4,0,3,2,1:T(8,128)(2,1)}, u32[]{:S(2)}, u32[]{:S(2)}) collective-permute-start(bf16[8,1,4,2,4096]{4,0,3,2,1:T(8,128)(2,1)} %copy.157), channel_id=1, source_target_pairs={{0,16},{16,0},{1,17},{17,1},{2,18},{18,2},{3,19},{19,3},{4,20},{20... | collective-permute-start | bytes 1572872 | tf_op jit(solution)/shard_map/ppermute | solution.py:240
  25.9 86.8 %collective-permute-start.1 = (bf16[8,1,4,2,4096]{4,0,3,2,1:T(8,128)(2,1)}, bf16[8,1,4,2,4096]{4,0,3,2,1:T(8,128)(2,1)}, u32[]{:S(2)}, u32[]{:S(2)}) collective-permute-start(bf16[8,1,4,2,4096]{4,0,3,2,1:T(8,128)(2,1)} %copy.159), channel_id=1, source_target_pairs={{0,16},{16,0},{1,17},{17,1},{2,18},{18,2},{3,19},{19,3},{4,20},{20... | collective-permute-start | bytes 1572872 | tf_op jit(solution)/shard_map/ppermute | solution.py:240
  101.1 9.3 %copy-start.4 = (bf16[8,1,4,2,4096]{4,3,2,1,0:T(2,128)(2,1)S(1)}, bf16[8,1,4,2,4096]{4,3,2,1,0:T(2,128)(2,1)}, u32[]{:S(2)}) copy-start(bf16[8,1,4,2,4096]{4,3,2,1,0:T(2,128)(2,1)} %get-tuple-element.12) | copy-start | bytes 1572868
  110.2 2.2 copy-start.3
  110.2 112.4 %reduce-scatter.7.cloned.1.call-start = ((), (), s32[]{:S(2)}) async-start(), calls=%async_computation.7 | async-start | bytes 557056 | tf_op jit(solution)/shard_map/reduce_scatter | solution.py:281
  110.8 14.6 %collective-permute-start.2 = (bf16[8,1,4,2,4096]{4,0,3,2,1:T(8,128)(2,1)S(1)}, bf16[8,1,4,2,4096]{4,0,3,2,1:T(8,128)(2,1)S(1)}, u32[]{:S(2)}, u32[]{:S(2)}) collective-permute-start(bf16[8,1,4,2,4096]{4,0,3,2,1:T(8,128)(2,1)S(1)} %copy.161), channel_id=1, source_target_pairs={{0,16},{16,0},{1,17},{17,1},{2,18},{18,2},{3,19},{19,3},{4,20},{20... | collective-permute-start | bytes 1572872 | tf_op jit(solution)/shard_map/ppermute | solution.py:240
  114.9 9.2 %copy-start.2 = (bf16[8,1,4,2,4096]{4,3,2,1,0:T(2,128)(2,1)S(1)}, bf16[8,1,4,2,4096]{4,3,2,1,0:T(2,128)(2,1)}, u32[]{:S(2)}) copy-start(bf16[8,1,4,2,4096]{4,3,2,1,0:T(2,128)(2,1)} %get-tuple-element.10) | copy-start | bytes 1572868
  124.0 1.0 copy-start.1
  124.0 157.3 %reduce-scatter.9.cloned.1.call-start = ((), (), s32[]{:S(2)}) async-start(), calls=%async_computation.8 | async-start | bytes 557056 | tf_op jit(solution)/shard_map/reduce_scatter | solution.py:281
  124.4 11.4 %collective-permute-start.3 = (bf16[8,1,4,2,4096]{4,0,3,2,1:T(8,128)(2,1)S(1)}, bf16[8,1,4,2,4096]{4,0,3,2,1:T(8,128)(2,1)S(1)}, u32[]{:S(2)}, u32[]{:S(2)}) collective-permute-start(bf16[8,1,4,2,4096]{4,0,3,2,1:T(8,128)(2,1)S(1)} %copy.163), channel_id=1, source_target_pairs={{0,16},{16,0},{1,17},{17,1},{2,18},{18,2},{3,19},{19,3},{4,20},{20... | collective-permute-start | bytes 1572872 | tf_op jit(solution)/shard_map/ppermute | solution.py:240
  135.4 204.5 %reduce-scatter.11.cloned.1.call-start = ((), (), s32[]{:S(2)}) async-start(), calls=%async_computation.9 | async-start | bytes 557056 | tf_op jit(solution)/shard_map/reduce_scatter | solution.py:281
Sparse Core Ops, SparseCore 0:
  110.3 53.4 reduce-scatter.4
  167.4 55.1 reduce-scatter.6
  226.2 55.1 reduce-scatter.8
  284.7 55.1 reduce-scatter.10
